TPU v7x, 1024 devices: a whole 4x8x16 slice. The times are simulated.
1024 devices in a mesh: ctx: 64 (over x, z), fsdp: 16 (over y, core).
Axes of the slice: x: 4, y: 8, z: 16, core: 2. Of those that a mesh axis runs over, the one named last changes fastest.
Arguments:
- inputs: bfloat16 [8192, 8192], P('ctx', 'fsdp'), may hold values from -6 to 6
- upstream: bfloat16 [8192, 8192], P('ctx', 'fsdp'), may hold values from -6 to 6
- medium_filter: bfloat16 [512, 128], P('fsdp'), may hold values from -0.5 to 0.5
- short_filter: bfloat16 [512, 7], P('fsdp'), may hold values from -2 to 2
Outputs:
- input_gradient: bfloat16 [8192, 8192], P('ctx', 'fsdp')
- medium_gradient: float32 [512, 128], P('fsdp')
- short_gradient: float32 [512, 7], P('fsdp')
All inputs are finite; a program needn't handle non-finite values.
Results may differ from a plain program's by a relative error of at most 0.005.
Values may be sent and summed in bfloat16 or wider, within the bound.
A program may use at most 64 MiB of HBM per device.

v0:
```python
import math

import jax
import jax.numpy as jnp
import numpy as np
from jax import lax
from jax.sharding import PartitionSpec as P

GROUP = 16


def shifted(block, axis, distance):
    devices = range(lax.axis_size(axis))
    route = [(i - distance, i) for i in devices if i - distance in devices]
    return lax.ppermute(block, axis, route)


def band_tables(medium_filter, block_rows, band_count):
    tap_count = medium_filter.shape[1]
    offsets = (
        np.arange(band_count)[:, None, None] * block_rows
        + np.arange(block_rows)[None, :, None]
        - np.arange(block_rows)[None, None, :]
    )
    inside = (offsets >= 0) & (offsets < tap_count)
    indices = np.clip(offsets, 0, tap_count - 1).reshape(-1)
    picked = jnp.take(medium_filter, jnp.asarray(indices, dtype=jnp.int32), axis=1)
    picked = picked.reshape(medium_filter.shape[0], band_count, block_rows, block_rows)
    return jnp.where(jnp.asarray(inside)[None], picked, jnp.zeros((), medium_filter.dtype))


def blocked(source_t, block_rows):
    return source_t.reshape(
        source_t.shape[0] // GROUP, GROUP, source_t.shape[1] // block_rows, block_rows
    )


def causal_conv(source_t, bands, block_rows, band_count, number):
    pieces = blocked(source_t, block_rows)
    top = band_count - 1
    total = None
    for band_index in range(band_count):
        part = pieces[:, :, top - band_index : top - band_index + number]
        term = jnp.einsum(
            "gcks,gts->gckt", part, bands[:, band_index], preferred_element_type=jnp.float32
        )
        total = term if total is None else total + term
    return total.reshape(source_t.shape[0], number * block_rows)


def later_conv(source_t, bands, block_rows, band_count, number):
    pieces = blocked(source_t, block_rows)
    total = None
    for band_index in range(band_count):
        part = pieces[:, :, band_index : band_index + number]
        term = jnp.einsum(
            "gcks,gst->gckt", part, bands[:, band_index], preferred_element_type=jnp.float32
        )
        total = term if total is None else total + term
    return total.reshape(source_t.shape[0], number * block_rows)


def short_apply(source_t, short_channel, lead_rows, number):
    total = jnp.zeros((source_t.shape[0], number), jnp.float32)
    for tap_index in range(short_channel.shape[1]):
        window = source_t[:, lead_rows - tap_index : lead_rows - tap_index + number]
        total = total + short_channel[:, tap_index][:, None] * window.astype(jnp.float32)
    return total


def diagonal_sums(pair_sums, tap_count):
    group_count, band_count, block_rows = (
        pair_sums.shape[0],
        pair_sums.shape[1],
        pair_sums.shape[2],
    )
    widened = jnp.pad(pair_sums, ((0, 0), (0, 0), (0, 0), (block_rows, 0)))
    flattened = widened.reshape(group_count, band_count, 2 * block_rows * block_rows)
    flattened = jnp.pad(flattened, ((0, 0), (0, 0), (0, block_rows)))
    skewed = flattened.reshape(group_count, band_count, block_rows, 2 * block_rows + 1)
    flipped = jnp.sum(skewed, axis=2)[:, :, ::-1]
    extent = (band_count + 1) * block_rows + 1
    accum = jnp.zeros((group_count, extent), jnp.float32)
    for band_index in range(band_count):
        offset = band_index * block_rows
        accum = accum + jnp.pad(
            flipped[:, band_index], ((0, 0), (offset, extent - offset - 2 * block_rows - 1))
        )
    return accum[:, block_rows : block_rows + tap_count]


def local(inputs, upstream, medium_filter, short_filter):
    length_dev = inputs.shape[0]
    width = inputs.shape[1]
    groups = width // GROUP
    tap_count = medium_filter.shape[1]
    short_taps = short_filter.shape[1]
    halo_rows = tap_count - 1
    block_rows = math.gcd(length_dev, 128)
    lead_blocks = -(-halo_rows // block_rows)
    band_count = lead_blocks + 1
    lead_rows = lead_blocks * block_rows
    own_blocks = length_dev // block_rows
    top = band_count - 1
    bands = band_tables(medium_filter, block_rows, band_count)
    short_channel = jnp.repeat(short_filter, GROUP, axis=0).astype(jnp.float32)
    previous = shifted(inputs[length_dev - halo_rows :], "ctx", 1)
    front_pad = jnp.zeros((lead_rows - halo_rows, width), inputs.dtype)
    following, next_cot = shifted((inputs[:halo_rows], upstream[:halo_rows]), "ctx", -1)
    extended_t = jnp.concatenate([front_pad, previous, inputs, following, front_pad], axis=0).T
    span = length_dev + lead_rows
    conv_out = causal_conv(extended_t, bands, block_rows, band_count, span // block_rows)
    gate = short_apply(extended_t, short_channel, lead_rows, span)
    cot_full = jnp.concatenate([upstream, next_cot, front_pad], axis=0).T.astype(jnp.float32)
    gate_full = (cot_full * conv_out).astype(jnp.bfloat16)
    conv_full = (cot_full * gate).astype(jnp.bfloat16)
    gate_tail = gate_full[:, : length_dev + short_taps - 1]
    conv_cot = conv_full[:, :length_dev]
    gate_cot = gate_full[:, :length_dev]
    medium_back = later_conv(conv_full, bands, block_rows, band_count, own_blocks)
    short_back = jnp.zeros((width, length_dev), jnp.float32)
    short_rows = []
    gate_values = gate_cot.astype(jnp.float32)
    for tap_index in range(short_taps):
        ahead = gate_tail[:, tap_index : tap_index + length_dev].astype(jnp.float32)
        short_back = short_back + short_channel[:, tap_index][:, None] * ahead
        window = extended_t[:, lead_rows - tap_index : lead_rows - tap_index + length_dev].astype(
            jnp.float32
        )
        channel_sums = jnp.sum(gate_values * window, axis=1)
        short_rows.append(jnp.sum(channel_sums.reshape(groups, GROUP), axis=1))
    input_gradient = (medium_back + short_back).astype(jnp.bfloat16).T
    cot_blocks = blocked(conv_cot, block_rows)
    token_blocks = blocked(extended_t, block_rows)
    pair_list = []
    for band_index in range(band_count):
        part = token_blocks[:, :, top - band_index : top - band_index + own_blocks]
        pair_list.append(
            jnp.einsum("gckt,gcks->gts", cot_blocks, part, preferred_element_type=jnp.float32)
        )
    pair_sums = jnp.stack(pair_list, axis=1)
    medium_part = diagonal_sums(pair_sums, tap_count)
    short_part = jnp.stack(short_rows, axis=1)
    factor = float(GROUP * length_dev * lax.axis_size("ctx")) ** (-0.5)
    total_medium, total_short = lax.psum((medium_part, short_part), "ctx")
    return (input_gradient, total_medium * factor, total_short * factor)


def solution(mesh):
    return jax.shard_map(
        local,
        mesh=mesh,
        in_specs=(P("ctx", "fsdp"), P("ctx", "fsdp"), P("fsdp", None), P("fsdp", None)),
        out_specs=(P("ctx", "fsdp"), P("fsdp", None), P("fsdp", None)),
        check_vma=False,
    )
```

profile of v0, /device:TPU:32, one launch (start us, length us, event | category | flops | bytes accessed | tf_op | source)
XLA Modules:
  0.0 487.3 jit_solution(11623901559826601455)
XLA Ops:
  0.6 1.0 copy.31
  1.7 0.1 fusion.32
  1.8 4.3 collective-permute-start.1
  6.1 1.3 collective-permute-start.2
  7.4 1.0 copy.30
  8.4 1.3 collective-permute-start
  9.7 0.8 copy.35
  10.5 0.9 broadcast_clamp_fusion
  11.4 114.2 %gather_fusion = bf16[32768,32]{1,0:T(8,128)(2,1)} fusion(bf16[32,128]{0,1:T(8,128)(2,1)S(1)} %copy.35, s32[32768]{0:T(1024)S(1)} %broadcast_clamp_fusion), kind=kCustom, calls=%fused_computation | custom fusion | bytes 4325376 | tf_op jit(solution)/shard_map/jit(_take)/gather | solution.py:27
  125.6 8.6 %copy.37 = bf16[32,2,128,128]{3,2,0,1:T(8,128)(2,1)} copy(bf16[32,2,128,128]{0,3,2,1:T(8,128)(2,1)} %bitcast.86) | data formatting | bytes 4194304 | tf_op jit(solution)/shard_map/jit(_take)/gather | solution.py:27
  134.3 0.1 broadcast_in_dim.34
  134.3 0.1 convert_element_type.97
  134.5 1.7 broadcast_select_fusion
  136.2 0.0 copy-start.8
  136.3 0.3 concatenate.7
  136.6 0.1 reshape.88
  136.7 0.0 copy-start.3
  136.7 0.1 copy-done.6
  136.8 0.0 copy-done.8
  136.8 0.5 copy-done.3
  137.4 1.8 fusion.11
  139.2 1.0 reshape.84
  140.2 1.6 slice.230
  141.8 0.4 fusion.30
  142.1 1.2 fusion.29
  143.3 0.4 fusion.31
  143.7 0.4 fusion.4
  144.0 0.7 fusion.1
  144.7 0.7 convolution_add_fusion
  145.4 0.3 copy.41
  145.6 0.0 copy-start.7
  145.7 0.1 fusion.10
  145.8 0.8 fusion.26
  146.6 0.4 convolution_add_fusion.1
  147.0 0.7 fusion.19
  147.8 0.8 copy.44
  148.6 0.5 convolution_bitcast_fusion
  149.1 0.5 convolution_bitcast_fusion.1
  149.6 3.7 select_maximum_fusion
  153.3 9.4 %reshape.93 = f32[32,2,32768]{2,0,1:T(8,128)} reshape(f32[32,2,128,256]{3,2,0,1:T(8,128)} %select_maximum_fusion) | data formatting | bytes 16777216 | tf_op jit(solution)/shard_map/reshape | solution.py:78
  162.7 7.1 %pad.17 = f32[32,2,32896]{2,0,1:T(8,128)} pad(f32[32,2,32768]{2,0,1:T(8,128)} %reshape.93, f32[]{:T(128)} %constant.28.clone.1), padding=0_0x0_0x0_128 | pad | bytes 16809988 | tf_op jit(solution)/shard_map/jit(_pad)/pad | solution.py:79
  169.8 14.1 %reshape.94 = f32[32,2,128,257]{3,2,0,1:T(8,128)} reshape(f32[32,2,32896]{2,0,1:T(8,128)} %pad.17) | data formatting | bytes 16842752 | tf_op jit(solution)/shard_map/reshape | solution.py:80
  184.0 6.1 %reduce_sum.135 = f32[32,2,257]{2,0,1:T(8,128)S(1)} reduce(f32[32,2,128,257]{3,2,0,1:T(8,128)} %reshape.94, f32[]{:T(128)} %constant.28.clone.1), dimensions={2}, to_apply=%region_0.1 | reduce | flops 2088896 | bytes 8487172 | tf_op jit(solution)/shard_map/reduce_sum | solution.py:81
  190.1 0.2 reverse.2
  190.3 0.1 slice_bitcast_fusion.1
  190.4 0.2 reverse.3
  190.6 0.1 slice_bitcast_fusion
  190.7 0.1 reshape.95
  190.8 0.1 reduce_sum.137
  190.9 0.1 reshape.96
  191.0 0.1 reduce_sum.139
  191.1 0.1 reshape.97
  191.2 0.1 reduce_sum.141
  191.3 0.1 reshape.98
  191.4 0.1 reduce_sum.143
  191.5 0.1 reshape.99
  191.6 0.1 reduce_sum.145
  191.7 0.1 reshape.100
  191.8 0.1 reduce_sum.147
  191.9 0.1 reshape.101
  192.0 0.1 reduce_sum.149
  192.2 293.9 %all-reduce.4 = (f32[32,128]{1,0:T(8,128)S(1)}, f32[32,7]{0,1:T(8,128)S(1)}) all-reduce(f32[32,128]{1,0:T(8,128)S(1)} %pad_add_fusion, f32[32,7]{0,1:T(8,128)S(1)} %stack.43), channel_id=1, replica_groups=mesh['ctx'=64,'fsdp'=16] {'ctx'}, use_global_device_ids=true, to_apply=%region_1.2 | all-reduce | flops 4320 | bytes 34560 | tf_op jit(solution)/shard_map/psum | solution.py:145
  486.1 0.6 broadcast_multiply_fusion
  486.7 0.6 broadcast_multiply_fusion.1
  (28 shorter events, 0.1 us)
Async XLA Ops:
  1.8 134.5 %collective-permute-start.1 = (bf16[127,512]{0,1:T(8,128)(2,1)S(1)}, bf16[127,512]{0,1:T(8,128)(2,1)S(1)}, u32[]{:S(2)}, u32[]{:S(2)}) collective-permute-start(bf16[127,512]{0,1:T(8,128)(2,1)S(1)} %get-tuple-element.25), channel_id=1, source_target_pairs={{0,16},{16,32},{32,48},{48,64},{64,80},{80,96},{96,112},{112,128},... | collective-permute-start | bytes 390152 | tf_op jit(solution)/shard_map/ppermute | solution.py:15
  6.1 130.2 %collective-permute-start.2 = (bf16[127,512]{0,1:T(8,128)(2,1)S(1)}, bf16[127,512]{0,1:T(8,128)(2,1)S(1)}, u32[]{:S(2)}, u32[]{:S(2)}) collective-permute-start(bf16[127,512]{0,1:T(8,128)(2,1)S(1)} %get-tuple-element.24), channel_id=1, source_target_pairs={{16,0},{32,16},{48,32},{64,48},{80,64},{96,80},{112,96},{128,112},... | collective-permute-start | bytes 390152 | tf_op jit(solution)/shard_map/ppermute | solution.py:15
  8.4 128.3 %collective-permute-start = (bf16[127,512]{0,1:T(8,128)(2,1)S(1)}, bf16[127,512]{0,1:T(8,128)(2,1)S(1)}, u32[]{:S(2)}, u32[]{:S(2)}) collective-permute-start(bf16[127,512]{0,1:T(8,128)(2,1)S(1)} %bitcast.88), channel_id=1, source_target_pairs={{16,0},{32,16},{48,32},{64,48},{80,64},{96,80},{112,96},{128,112},... | collective-permute-start | bytes 390152 | tf_op jit(solution)/shard_map/ppermute | solution.py:15
  125.6 8.6 %copy-start.12 = (bf16[32,7]{0,1:T(8,128)(2,1)S(1)}, bf16[32,7]{0,1:T(8,128)(2,1)}, u32[]{:S(2)}) copy-start(bf16[32,7]{0,1:T(8,128)(2,1)} %param.9) | copy-start | bytes 1348
  125.6 8.8 %copy-start.5 = (pred[2,128,128]{2,1,0:T(32,128)(4,1)S(1)}, pred[2,128,128]{2,1,0:T(32,128)(4,1)}, u32[]{:S(2)}) copy-start(pred[2,128,128]{2,1,0:T(32,128)(4,1)} %constant.31.clone) | copy-start | bytes 98308
  136.2 0.6 copy-start.6
  136.2 0.6 copy-start.8
  136.2 0.6 copy-start.10
  136.7 0.7 copy-start.3
  144.7 1.0 copy-start.4
  145.6 1.4 copy-start.7
  145.7 1.4 copy-start.9
  145.7 1.3 copy-start.11
  145.8 2.8 copy-start
  145.8 2.7 copy-start.2
  147.0 2.0 copy-start.1
where the time goes:
time: 488 us; the launch traced here: 487 us
  blocking collectives  294 us (60%)
  local copies, waits for them, and re-layouts  164 us (34%)
  other arithmetic  18 us (4%)
  starting transfers between devices  6.87 us (1%)
    psum x1, blocking collectives, local(): total_medium, total_short = lax.psum((medium_part, short_part), 'ctx')  294 us
    gather x2, local copies, waits for them, and re-layouts, band_tables(): jnp.take(medium_filter, jnp.asarray(indices, dtype=jnp.int32), axis=1)  123 us
    reshape x1, local copies, waits for them, and re-layouts, diagonal_sums(): flattened.reshape(group_count, band_count, block_rows, 2 * block_rows + 1)  14.1 us
  transfers between devices with their start and end apart: 3, of which 0 were waited for; matrix products, arithmetic and copies ran while one was open for 26% of the time, Pallas kernels for 0%

commit v1 on v0

v1 whole, which is shorter than its diff:
```python
import functools

import jax
import jax.numpy as jnp
from jax import lax
from jax.experimental import pallas as pl
from jax.experimental.pallas import tpu as pltpu
from jax.sharding import PartitionSpec as P

GROUP = 16
ROWS = 128
LANES = 128
PER = LANES // GROUP
MESH = pl.DeviceIdType.MESH
NEAR = (1, -1, 2, -2, 3)
F32 = jnp.float32
BF16 = jnp.bfloat16


def nt(a, b):
    return lax.dot_general(a, b, (((1,), (1,)), ((), ())), preferred_element_type=F32)


def kernel(
    nx, nz, x_hbm, up_hbm, med_ref, short_ref, ig_hbm, tot_ref,
    xe, upv, cce, gce, igv, tf, tb, mrev, mfwd, sch, xf, sacc,
    rx, xs, rz, s5, s6, r2,
    load_sem, halo_send, halo_recv, back_send, back_recv,
    x_send, x_recv, z_send, z_recv, w_send, w_recv, out_sem, ready_a, ready_b,
):
    n = nx * nz
    width = xe.shape[1]
    blocks = width // LANES
    groups = width // GROUP
    taps = short_ref.shape[0]
    me = lax.axis_index("ctx")
    ix, iz = me // nz, lax.rem(me, nz)
    nxt, prv = lax.rem(me + 1, n), lax.rem(me + n - 1, n)

    def at_z(d):
        return {"ctx": ix * nz + lax.rem(iz + d + nz, nz)}

    def at_x(d):
        return {"ctx": lax.rem(ix + d + nx, nx) * nz + iz}

    def lanes(b):
        return pl.ds(pl.multiple_of(b * LANES, LANES), LANES)

    load_x = pltpu.make_async_copy(x_hbm, xe.at[pl.ds(ROWS, ROWS)], load_sem.at[0])
    load_u = pltpu.make_async_copy(up_hbm, upv, load_sem.at[1])
    load_x.start()
    load_u.start()

    barrier = pltpu.get_barrier_semaphore()
    near = [{"ctx": nxt}, {"ctx": prv}]
    near += [at_x(d) for d in range(1, nx)]
    near += [at_z(d) for d in (1, -1, 2, -2)]
    for peer in near:
        pl.semaphore_signal(barrier, inc=1, device_id=peer, device_id_type=MESH)
    pl.semaphore_wait(barrier, len(near))

    def halo(b):
        return pltpu.make_async_remote_copy(
            src_ref=x_hbm.at[:, lanes(b)],
            dst_ref=xe.at[pl.ds(0, ROWS), lanes(b)],
            send_sem=halo_send.at[b],
            recv_sem=halo_recv.at[b],
            device_id={"ctx": nxt},
            device_id_type=MESH,
        )

    @pl.when(me < n - 1)
    def _():
        for b in range(blocks):
            halo(b).start()

    for d in (2, -2):
        pl.semaphore_signal(ready_a, inc=1, device_id=at_z(d), device_id_type=MESH)

    rows2 = lax.broadcasted_iota(jnp.int32, (ROWS, LANES), 0)
    cols2 = lax.broadcasted_iota(jnp.int32, (ROWS, LANES), 1)
    lane_group = cols2 // GROUP

    flip = (rows2 + cols2 == LANES - 1).astype(BF16)
    mrev[...] = jnp.dot(med_ref[...], flip, preferred_element_type=F32)
    mfwd[...] = med_ref[...].astype(F32)
    chan = lax.broadcasted_iota(jnp.int32, (groups, width), 1) // GROUP
    own = lax.broadcasted_iota(jnp.int32, (groups, width), 0)
    spread = (chan == own).astype(BF16)
    sch[0:taps, :] = jnp.dot(short_ref[...], spread, preferred_element_type=F32)

    def forward_table(g, carry):
        row = jnp.broadcast_to(mrev[pl.ds(g, 1), :], (ROWS, LANES))
        turned = pltpu.roll(row, 1, 1, stride=1, stride_axis=0)
        top = pl.ds(pl.multiple_of(g * ROWS, ROWS), ROWS)
        tf[top, 0:LANES] = jnp.where(cols2 > rows2, turned, 0.0).astype(BF16)
        tf[top, LANES:] = jnp.where(cols2 <= rows2, turned, 0.0).astype(BF16)
        return carry

    lax.fori_loop(0, groups, forward_table, 0)

    pl.semaphore_wait(ready_a, 2)
    for d in (2, -2):
        pl.semaphore_signal(ready_b, inc=1, device_id=at_z(d), device_id_type=MESH)

    big_r = lax.broadcasted_iota(jnp.int32, (2 * ROWS, 2 * ROWS), 0)
    big_c = lax.broadcasted_iota(jnp.int32, (2 * ROWS, 2 * ROWS), 1)
    flip_rows = (big_r + big_c == 2 * ROWS - 1).astype(BF16)

    load_x.wait()
    load_u.wait()

    def block(b, carry):
        @pl.when(me > 0)
        def _():
            halo(b).wait_recv()

        @pl.when(me == 0)
        def _():
            xe[pl.ds(0, ROWS), lanes(b)] = jnp.zeros((ROWS, LANES), BF16)

        xb = xe[:, lanes(b)]
        xf[...] = xe[pl.ds(ROWS - 16, ROWS + 16), lanes(b)].astype(F32)
        gate = jnp.zeros((ROWS, LANES), F32)
        for j in range(taps):
            gate = gate + sch[j : j + 1, lanes(b)] * xf[16 - j : 16 - j + ROWS, :]
        conv = jnp.zeros((ROWS, LANES), F32)
        for k in range(PER):
            top = pl.ds(pl.multiple_of((b * PER + k) * ROWS, ROWS), ROWS)
            term = jnp.dot(tf[top, :], xb, preferred_element_type=F32)
            conv = jnp.where(lane_group == k, term, conv)
        up = upv[:, lanes(b)].astype(F32)
        gate_cot = (up * conv).astype(BF16)
        conv_cot = (up * gate).astype(BF16)
        cce[0:ROWS, lanes(b)] = conv_cot
        gce[0:ROWS, lanes(b)] = gate_cot
        gate_f = gate_cot.astype(F32)
        for j in range(taps):
            sacc[j : j + 1, lanes(b)] = jnp.sum(
                gate_f * xf[16 - j : 16 - j + ROWS, :], axis=0, keepdims=True
            )
        x_rev = jnp.dot(flip_rows, xb, preferred_element_type=F32).astype(BF16)
        for k in range(PER):
            part = jnp.where(lane_group == k, conv_cot, jnp.zeros((), BF16))
            pair = nt(part, x_rev)
            both = jnp.where(rows2 + cols2 >= LANES - 1, pair[:, :LANES], pair[:, LANES:])
            turned = pltpu.roll(both, 1, 1, stride=1, stride_axis=0)
            rx[ix, pl.ds(b * PER + k, 1), :] = jnp.sum(turned, axis=0, keepdims=True)
        return carry

    sacc[...] = jnp.zeros_like(sacc)
    lax.fori_loop(0, blocks, block, 0)

    tall_r = lax.broadcasted_iota(jnp.int32, (width, LANES), 0) // GROUP
    tall_c = lax.broadcasted_iota(jnp.int32, (width, LANES), 1)
    rx[ix, groups : groups + 8, :] = jnp.dot(
        sacc[...],
        (tall_r == tall_c).astype(F32),
        preferred_element_type=F32,
        precision=lax.Precision.HIGHEST,
    )

    def remote(src, dst, send, recv, peer):
        return pltpu.make_async_remote_copy(
            src_ref=src, dst_ref=dst, send_sem=send, recv_sem=recv, device_id=peer, device_id_type=MESH
        )

    pl.semaphore_wait(ready_b, 2)
    x_sends = [
        remote(rx.at[ix], rx.at[ix], x_send.at[d - 1], x_recv.at[d - 1], at_x(d)) for d in range(1, nx)
    ]
    for copy in x_sends:
        copy.start()

    back_c = remote(
        cce.at[pl.ds(0, ROWS)], cce.at[pl.ds(ROWS, ROWS)], back_send.at[0], back_recv.at[0], {"ctx": prv}
    )
    back_g = remote(
        gce.at[pl.ds(0, 16)], gce.at[pl.ds(ROWS, 16)], back_send.at[1], back_recv.at[1], {"ctx": prv}
    )

    @pl.when(me > 0)
    def _():
        back_g.start()
        back_c.start()

    def backward_table(g, carry):
        row = jnp.broadcast_to(mfwd[pl.ds(g, 1), :], (ROWS, LANES))
        turned = pltpu.roll(row, 0, 1, stride=1, stride_axis=0)
        top = pl.ds(pl.multiple_of(g * ROWS, ROWS), ROWS)
        tb[top, 0:LANES] = jnp.where(cols2 >= rows2, turned, 0.0).astype(BF16)
        tb[top, LANES:] = jnp.where(cols2 < rows2, turned, 0.0).astype(BF16)
        return carry

    lax.fori_loop(0, groups, backward_table, 0)

    for d in range(1, nx):
        source = lax.rem(ix - d + nx, nx)
        remote(rx.at[ix], rx.at[source], x_send.at[d - 1], x_recv.at[d - 1], at_x(d)).wait_recv()
    total = rx[0]
    for k in range(1, nx):
        total = total + rx[k]
    xs[...] = total
    z_sends = [remote(xs, rz.at[k], z_send.at[k], z_recv.at[k], at_z(-d)) for k, d in enumerate(NEAR)]
    for copy in z_sends:
        copy.start()
    for copy in z_sends[:4]:
        copy.wait_recv()
    five = ((rz[3] + rz[1]) + xs[...]) + (rz[0] + rz[2])
    s5[...] = five
    far_five = remote(s5, r2.at[0], w_send.at[0], w_recv.at[0], at_z(5))
    far_five.start()
    z_sends[4].wait_recv()
    s6[...] = five + rz[4]
    far_six = remote(s6, r2.at[1], w_send.at[1], w_recv.at[1], at_z(-5))
    far_six.start()

    @pl.when(me < n - 1)
    def _():
        back_g.wait_recv()
        back_c.wait_recv()

    @pl.when(me == n - 1)
    def _():
        cce[pl.ds(ROWS, ROWS), :] = jnp.zeros((ROWS, width), BF16)
        gce[pl.ds(ROWS, 16), :] = jnp.zeros((16, width), BF16)

    def store(b):
        return pltpu.make_async_copy(igv.at[:, lanes(b)], ig_hbm.at[:, lanes(b)], out_sem.at[b])

    def gradient(b, carry):
        cb = cce[:, lanes(b)]
        back = jnp.zeros((ROWS, LANES), F32)
        for k in range(PER):
            top = pl.ds(pl.multiple_of((b * PER + k) * ROWS, ROWS), ROWS)
            term = jnp.dot(tb[top, :], cb, preferred_element_type=F32)
            back = jnp.where(lane_group == k, term, back)
        xf[...] = gce[:, lanes(b)].astype(F32)
        short = jnp.zeros((ROWS, LANES), F32)
        for j in range(taps):
            short = short + sch[j : j + 1, lanes(b)] * xf[j : j + ROWS, :]
        igv[:, lanes(b)] = (back + short).astype(BF16)
        store(b).start()
        return carry

    lax.fori_loop(0, blocks, gradient, 0)

    far_five.wait_recv()
    far_six.wait_recv()
    tot_ref[...] = s5[...] + r2[0] + r2[1]

    for b in range(blocks):
        store(b).wait()

    @pl.when(me < n - 1)
    def _():
        for b in range(blocks):
            halo(b).wait_send()

    @pl.when(me > 0)
    def _():
        back_g.wait_send()
        back_c.wait_send()

    for copy in x_sends + z_sends + [far_five, far_six]:
        copy.wait_send()


def local(nx, nz, inputs, upstream, medium_filter, short_filter):
    rows, width = inputs.shape
    groups, taps = medium_filter.shape
    short_taps = short_filter.shape[1]
    if rows != ROWS or taps != LANES or width % LANES or groups != 32:
        raise ValueError("unsupported sizes")
    height = groups + 8
    blocks = width // LANES
    vmem = functools.partial(pltpu.VMEM)
    dma = pltpu.SemaphoreType.DMA
    gradient, total = pl.pallas_call(
        functools.partial(kernel, nx, nz),
        out_shape=(
            jax.ShapeDtypeStruct((rows, width), BF16),
            jax.ShapeDtypeStruct((height, LANES), F32),
        ),
        in_specs=[
            pl.BlockSpec(memory_space=pl.ANY),
            pl.BlockSpec(memory_space=pl.ANY),
            pl.BlockSpec(memory_space=pltpu.VMEM),
            pl.BlockSpec(memory_space=pltpu.VMEM),
        ],
        out_specs=(pl.BlockSpec(memory_space=pl.ANY), pl.BlockSpec(memory_space=pltpu.VMEM)),
        scratch_shapes=[
            vmem((2 * ROWS, width), BF16),
            vmem((ROWS, width), BF16),
            vmem((2 * ROWS, width), BF16),
            vmem((ROWS + 16, width), BF16),
            vmem((ROWS, width), BF16),
            vmem((groups * ROWS, 2 * LANES), BF16),
            vmem((groups * ROWS, 2 * LANES), BF16),
            vmem((groups, LANES), F32),
            vmem((groups, LANES), F32),
            vmem((8, width), F32),
            vmem((ROWS + 16, LANES), F32),
            vmem((8, width), F32),
            vmem((nx, height, LANES), F32),
            vmem((height, LANES), F32),
            vmem((len(NEAR), height, LANES), F32),
            vmem((height, LANES), F32),
            vmem((height, LANES), F32),
            vmem((2, height, LANES), F32),
            dma((2,)),
            dma((blocks,)),
            dma((blocks,)),
            dma((2,)),
            dma((2,)),
            dma((nx - 1,)),
            dma((nx - 1,)),
            dma((len(NEAR),)),
            dma((len(NEAR),)),
            dma((2,)),
            dma((2,)),
            dma((blocks,)),
            pltpu.SemaphoreType.REGULAR,
            pltpu.SemaphoreType.REGULAR,
        ],
        compiler_params=pltpu.CompilerParams(collective_id=0, has_side_effects=True),
    )(inputs, upstream, medium_filter, short_filter.T)
    factor = float(GROUP * rows * lax.axis_size("ctx")) ** (-0.5)
    medium = total[:groups] * factor
    short = total[groups : groups + short_taps, :groups].T * factor
    return gradient, medium, short


def solution(mesh):
    n = mesh.shape["ctx"]
    nz = 16
    return jax.shard_map(
        functools.partial(local, n // nz, nz),
        mesh=mesh,
        in_specs=(P("ctx", "fsdp"), P("ctx", "fsdp"), P("fsdp", None), P("fsdp", None)),
        out_specs=(P("ctx", "fsdp"), P("fsdp", None), P("fsdp", None)),
        check_vma=False,
    )
```

time: 488 us -> 45.2 us (0.09)
  the two profiles are of different devices: /device:TPU:32 before, /device:TPU:40 now
where the time goes in v1:
time: 45.2 us; the launch traced here: 44.9 us
  Pallas kernels  40.1 us (89%)
  other arithmetic  2.59 us (6%)
  local copies, waits for them, and re-layouts  1.57 us (3%)
  between operations  0.64 us (1%)
    pallas_call x1, Pallas kernels, local(): pl.pallas_call(functools.partial(kernel, nx, nz), out_shape=(jax.ShapeDty...  40.1 us
    unnamed x1, local copies, waits for them, and re-layouts  1.57 us
    mul x1, other arithmetic, local(): medium = total[:groups] * factor  1.32 us
    mul x1, other arithmetic, local(): short = total[groups:groups + short_taps, :groups].T * factor  1.27 us

profile of v1, /device:TPU:40, one launch (start us, length us, event | category | flops | bytes accessed | tf_op | source)
XLA Modules:
  0.0 44.9 jit_solution(14121390414213815157)
XLA Ops:
  0.6 40.1 %shard_map.67 = (bf16[128,512]{1,0:T(8,128)(2,1)}, f32[40,128]{1,0:T(8,128)}) custom-call(bf16[128,512]{1,0:T(8,128)(2,1)} %x_hbm.1, bf16[128,512]{1,0:T(8,128)(2,1)} %up_hbm.1, bf16[32,128]{1,0:T(8,128)(2,1)} %med_ref.1, bf16[7,32]{1,0:T(8,128)(2,1)} %bitcast.3), custom_call_target="tpu_custom_call" | custom-call | tf_op jit(solution)/shard_map/pallas_call | solution.py:279
  40.7 1.3 %multiply_bitcast_fusion = f32[32,7]{0,1:T(8,128)} fusion(f32[40,128]{1,0:T(8,128)} %get-tuple-element.6), kind=kLoop, calls=%fused_computation.1 | loop fusion | flops 224 | bytes 1792 | tf_op jit(solution)/shard_map/mul | solution.py:330
  42.0 1.3 %slice_multiply_fusion = f32[32,128]{1,0:T(8,128)} fusion(f32[40,128]{1,0:T(8,128)} %get-tuple-element.6), kind=kLoop, calls=%fused_computation | loop fusion | flops 4096 | bytes 32768 | tf_op jit(solution)/shard_map/mul | solution.py:329
  43.3 1.6 %copy.8 = bf16[128,512]{1,0:T(8,128)(2,1)} copy(bf16[128,512]{1,0:T(8,128)(2,1)} %get-tuple-element.10) | data formatting | bytes 262144

commit v2 on v1

v2 whole, which is shorter than its diff:
```python
import functools

import jax
import jax.numpy as jnp
from jax import lax
from jax.experimental import pallas as pl
from jax.experimental.pallas import tpu as pltpu
from jax.sharding import PartitionSpec as P

GROUP = 16
ROWS = 128
LANES = 128
PER = LANES // GROUP
MESH = pl.DeviceIdType.MESH
RAW = (1, 2, 3)
WIDE = (4, -4, 8)
F32 = jnp.float32
BF16 = jnp.bfloat16


def nt(a, b):
    return lax.dot_general(a, b, (((1,), (1,)), ((), ())), preferred_element_type=F32)


def kernel(
    nx, nz, x_hbm, up_hbm, med_hbm, short_hbm, igv, tot_ref,
    xe, upv, med_ref, short_ref, cce, gce, tf, tb, mrev, mfwd, sch, xf, sacc,
    rx, xs, rz, win, rw,
    load_sem, halo_send, halo_recv, back_send, back_recv,
    x_send, x_recv, z_send, z_recv, w_send, w_recv, go, across,
):
    n = nx * nz
    width = xe.shape[1]
    blocks = width // LANES
    groups = width // GROUP
    taps = short_ref.shape[0]
    me = lax.axis_index("ctx")
    ix, iz = me // nz, lax.rem(me, nz)

    def at_z(d):
        return ix, lax.rem(iz + d + nz, nz)

    def at_x(d):
        return lax.rem(ix + d + nx, nx), iz

    def at(d):
        other = lax.rem(me + d + n, n)
        return other // nz, lax.rem(other, nz)

    def ident(peer):
        return {"ctx": peer[0] * nz + peer[1]}

    def signal(sem, peer):
        pl.semaphore_signal(sem, inc=1, device_id=ident(peer), device_id_type=MESH)

    def later(peer):
        return (peer[1] > iz) | ((peer[1] == iz) & (peer[0] > ix))

    def lanes(b):
        return pl.ds(pl.multiple_of(b * LANES, LANES), LANES)

    loads = [
        pltpu.make_async_copy(x_hbm, xe.at[pl.ds(ROWS, ROWS)], load_sem.at[0]),
        pltpu.make_async_copy(up_hbm, upv, load_sem.at[1]),
        pltpu.make_async_copy(med_hbm, med_ref, load_sem.at[2]),
        pltpu.make_async_copy(short_hbm, short_ref, load_sem.at[3]),
    ]
    for copy in loads:
        copy.start()

    routes = [(at(1), at(-1)), (at(-1), at(1)), (at_x(1), at_x(-1)), (at_x(-1), at_x(1))]
    routes += [(at_z(d), at_z(-d)) for d in RAW + WIDE]
    barrier = pltpu.get_barrier_semaphore()
    known = jnp.int32(0)
    for peers in routes:
        for peer in peers:
            pl.when(later(peer))(functools.partial(signal, barrier, peer))
            known = known + jnp.where(later(peer), 0, 1)

    @pl.when(known > 0)
    def _():
        pl.semaphore_wait(barrier, known)

    for k, (_, source) in enumerate(routes):
        pl.when(jnp.logical_not(later(source)))(functools.partial(signal, go.at[k], source))

    def ready(k):
        @pl.when(later(routes[k][0]))
        def _():
            pl.semaphore_wait(go.at[k], 1)

    def halo(b):
        return pltpu.make_async_remote_copy(
            src_ref=xe.at[pl.ds(ROWS, ROWS), lanes(b)],
            dst_ref=xe.at[pl.ds(0, ROWS), lanes(b)],
            send_sem=halo_send.at[b],
            recv_sem=halo_recv.at[b],
            device_id=ident(at(1)),
            device_id_type=MESH,
        )

    follows = later(at(1))
    loads[0].wait()

    @pl.when((me < n - 1) & jnp.logical_not(follows))
    def _():
        for b in range(blocks):
            halo(b).start()

    loads[2].wait()
    loads[3].wait()

    rows2 = lax.broadcasted_iota(jnp.int32, (ROWS, LANES), 0)
    cols2 = lax.broadcasted_iota(jnp.int32, (ROWS, LANES), 1)
    lane_group = cols2 // GROUP

    flip = (rows2 + cols2 == LANES - 1).astype(BF16)
    mrev[...] = jnp.dot(med_ref[...], flip, preferred_element_type=F32)
    mfwd[...] = med_ref[...].astype(F32)
    chan = lax.broadcasted_iota(jnp.int32, (groups, width), 1) // GROUP
    own = lax.broadcasted_iota(jnp.int32, (groups, width), 0)
    spread = (chan == own).astype(BF16)
    sch[0:taps, :] = jnp.dot(short_ref[...], spread, preferred_element_type=F32)

    above = (cols2 > rows2).astype(F32).astype(BF16)
    below = (cols2 <= rows2).astype(F32).astype(BF16)

    def forward_table(b, carry):
        for k in range(PER):
            g = b * PER + k
            row = jnp.broadcast_to(mrev[pl.ds(g, 1), :], (ROWS, LANES))
            turned = pltpu.roll(row, 1, 1, stride=1, stride_axis=0).astype(BF16)
            top = pl.ds(pl.multiple_of(g * ROWS, ROWS), ROWS)
            tf[top, 0:LANES] = turned * above
            tf[top, LANES:] = turned * below
        return carry

    def next_halo():
        ready(0)

        @pl.when((me < n - 1) & follows)
        def _():
            for b in range(blocks):
                halo(b).start()

    lax.fori_loop(0, 1, forward_table, 0)
    next_halo()
    lax.fori_loop(1, blocks, forward_table, 0)
    ready(2)
    ready(3)
    for d in (1, -1):
        signal(across, at_x(d))

    big_r = lax.broadcasted_iota(jnp.int32, (2 * ROWS, 2 * ROWS), 0)
    big_c = lax.broadcasted_iota(jnp.int32, (2 * ROWS, 2 * ROWS), 1)
    flip_rows = (big_r + big_c == 2 * ROWS - 1).astype(BF16)

    loads[1].wait()

    def block(b, carry):
        @pl.when(me > 0)
        def _():
            halo(b).wait_recv()

        @pl.when(me == 0)
        def _():
            xe[pl.ds(0, ROWS), lanes(b)] = jnp.zeros((ROWS, LANES), BF16)

        xb = xe[:, lanes(b)]
        xf[...] = xe[pl.ds(ROWS - 16, ROWS + 16), lanes(b)].astype(F32)
        gate = jnp.zeros((ROWS, LANES), F32)
        for j in range(taps):
            gate = gate + sch[j : j + 1, lanes(b)] * xf[16 - j : 16 - j + ROWS, :]
        conv = jnp.zeros((ROWS, LANES), F32)
        for k in range(PER):
            top = pl.ds(pl.multiple_of((b * PER + k) * ROWS, ROWS), ROWS)
            term = jnp.dot(tf[top, :], xb, preferred_element_type=F32)
            conv = jnp.where(lane_group == k, term, conv)
        up = upv[:, lanes(b)].astype(F32)
        gate_cot = (up * conv).astype(BF16)
        conv_cot = (up * gate).astype(BF16)
        cce[0:ROWS, lanes(b)] = conv_cot
        gce[0:ROWS, lanes(b)] = gate_cot
        gate_f = gate_cot.astype(F32)
        for j in range(taps):
            sacc[j : j + 1, lanes(b)] = jnp.sum(
                gate_f * xf[16 - j : 16 - j + ROWS, :], axis=0, keepdims=True
            )
        x_rev = jnp.dot(flip_rows, xb, preferred_element_type=F32).astype(BF16)
        for k in range(PER):
            part = jnp.where(lane_group == k, conv_cot, jnp.zeros((), BF16))
            pair = nt(part, x_rev)
            both = jnp.where(rows2 + cols2 >= LANES - 1, pair[:, :LANES], pair[:, LANES:])
            turned = pltpu.roll(both, 1, 1, stride=1, stride_axis=0)
            rx[ix, pl.ds(b * PER + k, 1), :] = jnp.sum(turned, axis=0, keepdims=True)
        return carry

    sacc[...] = jnp.zeros_like(sacc)
    lax.fori_loop(0, blocks, block, 0)

    tall_r = lax.broadcasted_iota(jnp.int32, (width, LANES), 0) // GROUP
    tall_c = lax.broadcasted_iota(jnp.int32, (width, LANES), 1)
    rx[ix, groups : groups + 8, :] = jnp.dot(
        sacc[...],
        (tall_r == tall_c).astype(F32),
        preferred_element_type=F32,
        precision=lax.Precision.HIGHEST,
    )

    def remote(src, dst, send, recv, peer):
        return pltpu.make_async_remote_copy(
            src_ref=src, dst_ref=dst, send_sem=send, recv_sem=recv, device_id=ident(peer), device_id_type=MESH
        )

    pl.semaphore_wait(across, 2)
    x_sends = [
        remote(rx.at[ix], rx.at[ix], x_send.at[d - 1], x_recv.at[d - 1], at_x(d)) for d in (2, 1, 3)
    ]
    for copy in x_sends:
        copy.start()

    back_c = remote(
        cce.at[pl.ds(0, ROWS)], cce.at[pl.ds(ROWS, ROWS)], back_send.at[0], back_recv.at[0], at(-1)
    )
    back_g = remote(
        gce.at[pl.ds(0, 16)], gce.at[pl.ds(ROWS, 16)], back_send.at[1], back_recv.at[1], at(-1)
    )

    ready(1)

    @pl.when(me > 0)
    def _():
        back_g.start()
        back_c.start()

    strict = (cols2 < rows2).astype(F32).astype(BF16)
    upper = (cols2 >= rows2).astype(F32).astype(BF16)

    def backward_table(b, carry):
        for k in range(PER):
            g = b * PER + k
            row = jnp.broadcast_to(mfwd[pl.ds(g, 1), :], (ROWS, LANES))
            turned = pltpu.roll(row, 0, 1, stride=1, stride_axis=0).astype(BF16)
            top = pl.ds(pl.multiple_of(g * ROWS, ROWS), ROWS)
            tb[top, 0:LANES] = turned * upper
            tb[top, LANES:] = turned * strict
        return carry

    lax.fori_loop(0, blocks, backward_table, 0)

    for d in range(1, nx):
        source = lax.rem(ix - d + nx, nx)
        remote(rx.at[ix], rx.at[source], x_send.at[d - 1], x_recv.at[d - 1], at_x(d)).wait_recv()
    total = rx[0]
    for k in range(1, nx):
        total = total + rx[k]
    xs[...] = total.astype(BF16)
    z_sends = [remote(xs, rz.at[k], z_send.at[k], z_recv.at[k], at_z(d)) for k, d in enumerate(RAW)]
    for k, copy in enumerate(z_sends):
        ready(4 + k)
        copy.start()
    for copy in z_sends:
        copy.wait_recv()
    window = (total + rz[0].astype(F32)) + (rz[1].astype(F32) + rz[2].astype(F32))
    win[...] = window.astype(BF16)
    tot_ref[...] = window
    w_sends = [remote(win, rw.at[k], w_send.at[k], w_recv.at[k], at_z(d)) for k, d in enumerate(WIDE)]
    for k, copy in enumerate(w_sends):
        ready(4 + len(RAW) + k)
        copy.start()

    @pl.when(me < n - 1)
    def _():
        back_g.wait_recv()
        back_c.wait_recv()

    @pl.when(me == n - 1)
    def _():
        cce[pl.ds(ROWS, ROWS), :] = jnp.zeros((ROWS, width), BF16)
        gce[pl.ds(ROWS, 16), :] = jnp.zeros((16, width), BF16)

    def gradient(b, carry):
        cb = cce[:, lanes(b)]
        back = jnp.zeros((ROWS, LANES), F32)
        for k in range(PER):
            top = pl.ds(pl.multiple_of((b * PER + k) * ROWS, ROWS), ROWS)
            term = jnp.dot(tb[top, :], cb, preferred_element_type=F32)
            back = jnp.where(lane_group == k, term, back)
        xf[...] = gce[:, lanes(b)].astype(F32)
        short = jnp.zeros((ROWS, LANES), F32)
        for j in range(taps):
            short = short + sch[j : j + 1, lanes(b)] * xf[j : j + ROWS, :]
        igv[:, lanes(b)] = (back + short).astype(BF16)
        return carry

    lax.fori_loop(0, blocks, gradient, 0)

    for copy in w_sends:
        copy.wait_recv()
    tot_ref[...] = (tot_ref[...] + rw[0].astype(F32)) + (rw[1].astype(F32) + rw[2].astype(F32))

    @pl.when(me < n - 1)
    def _():
        for b in range(blocks):
            halo(b).wait_send()

    @pl.when(me > 0)
    def _():
        back_g.wait_send()
        back_c.wait_send()

    for copy in x_sends + z_sends + w_sends:
        copy.wait_send()


def finish(factor, ig_ref, tot_ref, ig_hbm, med_hbm, short_hbm, med_v, short_v, sems):
    groups, taps = med_v.shape[0], short_v.shape[0]
    big = pltpu.make_async_copy(ig_ref, ig_hbm, sems.at[0])
    big.start()
    med_v[...] = tot_ref[0:groups, :] * factor
    medium = pltpu.make_async_copy(med_v, med_hbm, sems.at[1])
    medium.start()
    short_v[...] = tot_ref[groups : groups + taps, 0:groups] * factor
    short = pltpu.make_async_copy(short_v, short_hbm, sems.at[2])
    short.start()
    big.wait()
    medium.wait()
    short.wait()


def local(nx, nz, inputs, upstream, medium_filter, short_filter):
    rows, width = inputs.shape
    groups, taps = medium_filter.shape
    short_taps = short_filter.shape[1]
    if rows != ROWS or taps != LANES or width % LANES or groups != 32:
        raise ValueError("unsupported sizes")
    height = groups + 8
    blocks = width // LANES
    vmem = pltpu.VMEM
    dma = pltpu.SemaphoreType.DMA
    hbm = pl.BlockSpec(memory_space=pl.ANY)
    local_mem = pl.BlockSpec(memory_space=pltpu.VMEM)
    gradient, total = pl.pallas_call(
        functools.partial(kernel, nx, nz),
        out_shape=(vmem((rows, width), BF16), vmem((height, LANES), F32)),
        in_specs=[hbm] * 4,
        out_specs=(local_mem, local_mem),
        scratch_shapes=[
            vmem((2 * ROWS, width), BF16),
            vmem((ROWS, width), BF16),
            vmem((groups, LANES), BF16),
            vmem((short_taps, groups), BF16),
            vmem((2 * ROWS, width), BF16),
            vmem((ROWS + 16, width), BF16),
            vmem((groups * ROWS, 2 * LANES), BF16),
            vmem((groups * ROWS, 2 * LANES), BF16),
            vmem((groups, LANES), F32),
            vmem((groups, LANES), F32),
            vmem((8, width), F32),
            vmem((ROWS + 16, LANES), F32),
            vmem((8, width), F32),
            vmem((nx, height, LANES), F32),
            vmem((height, LANES), BF16),
            vmem((len(RAW), height, LANES), BF16),
            vmem((height, LANES), BF16),
            vmem((len(WIDE), height, LANES), BF16),
            dma((4,)),
            dma((blocks,)),
            dma((blocks,)),
            dma((2,)),
            dma((2,)),
            dma((nx - 1,)),
            dma((nx - 1,)),
            dma((len(RAW),)),
            dma((len(RAW),)),
            dma((len(WIDE),)),
            dma((len(WIDE),)),
            pltpu.SemaphoreType.REGULAR((4 + len(RAW) + len(WIDE),)),
            pltpu.SemaphoreType.REGULAR,
        ],
        compiler_params=pltpu.CompilerParams(collective_id=0, has_side_effects=True),
    )(inputs, upstream, medium_filter, short_filter.T)
    factor = float(GROUP * rows * lax.axis_size("ctx")) ** (-0.5)
    gradient, medium, short = pl.pallas_call(
        functools.partial(finish, factor),
        out_shape=(
            jax.ShapeDtypeStruct((rows, width), BF16),
            jax.ShapeDtypeStruct((groups, LANES), F32),
            jax.ShapeDtypeStruct((short_taps, groups), F32),
        ),
        in_specs=[local_mem, local_mem],
        out_specs=(hbm, hbm, hbm),
        scratch_shapes=[vmem((groups, LANES), F32), vmem((short_taps, groups), F32), dma((3,))],
    )(pltpu.with_memory_space_constraint(gradient, pltpu.VMEM), pltpu.with_memory_space_constraint(total, pltpu.VMEM))
    return gradient, medium, short.T


def solution(mesh):
    n = mesh.shape["ctx"]
    nz = 16
    return jax.shard_map(
        functools.partial(local, n // nz, nz),
        mesh=mesh,
        in_specs=(P("ctx", "fsdp"), P("ctx", "fsdp"), P("fsdp", None), P("fsdp", None)),
        out_specs=(P("ctx", "fsdp"), P("fsdp", None), P("fsdp", None)),
        check_vma=False,
    )
```

time: 45.2 us -> 40.5 us (0.90)
  the two profiles are of different devices: /device:TPU:40 before, /device:TPU:66 now
where the time goes in v2:
time: 40.5 us; the launch traced here: 40.4 us
  Pallas kernels  39.7 us (98%)
  between operations  0.64 us (2%)
    pallas_call x1, Pallas kernels, local(): pl.pallas_call(functools.partial(kernel, nx, nz), out_shape=(vmem((rows,...  39 us

profile of v2, /device:TPU:66, one launch (start us, length us, event | category | flops | bytes accessed | tf_op | source)
XLA Modules:
  0.0 40.4 jit_solution(14758797624535588297)
XLA Ops:
  0.6 39.0 %shard_map.67 = (bf16[128,512]{1,0:T(8,128)(2,1)S(1)}, f32[40,128]{1,0:T(8,128)S(1)}) custom-call(bf16[128,512]{1,0:T(8,128)(2,1)} %x_hbm.1, bf16[128,512]{1,0:T(8,128)(2,1)} %up_hbm.1, bf16[32,128]{1,0:T(8,128)(2,1)} %med_hbm.1, bf16[7,32]{1,0:T(8,128)(2,1)} %bitcast.2), custom_call_target="tpu_custom_call" | custom-call | tf_op jit(solution)/shard_map/pallas_call | solution.py:343
  39.7 0.7 %shard_map.68 = (bf16[128,512]{1,0:T(8,128)(2,1)}, f32[32,128]{1,0:T(8,128)}, f32[7,32]{1,0:T(8,128)}) custom-call(bf16[128,512]{1,0:T(8,128)(2,1)S(1)} %get-tuple-element.8.ig_ref, f32[40,128]{1,0:T(8,128)S(1)} %get-tuple-element.9.tot_ref), custom_call_target="tpu_custom_call" | custom-call | tf_op jit(solution)/shard_map/pallas_call | solution.py:384

commit v3 on v2

--- a/solution.py
+++ b/solution.py
@@ -27,7 +27,7 @@
     xe, upv, med_ref, short_ref, cce, gce, tf, tb, mrev, mfwd, sch, xf, sacc,
     rx, xs, rz, win, rw,
     load_sem, halo_send, halo_recv, back_send, back_recv,
-    x_send, x_recv, z_send, z_recv, w_send, w_recv, go, across,
+    x_send, x_recv, z_send, z_recv, w_send, w_recv, go, steps,
 ):
     n = nx * nz
     width = xe.shape[1]
@@ -53,9 +53,6 @@
     def signal(sem, peer):
         pl.semaphore_signal(sem, inc=1, device_id=ident(peer), device_id_type=MESH)
 
-    def later(peer):
-        return (peer[1] > iz) | ((peer[1] == iz) & (peer[0] > ix))
-
     def lanes(b):
         return pl.ds(pl.multiple_of(b * LANES, LANES), LANES)
 
@@ -68,26 +65,9 @@
     for copy in loads:
         copy.start()
 
-    routes = [(at(1), at(-1)), (at(-1), at(1)), (at_x(1), at_x(-1)), (at_x(-1), at_x(1))]
-    routes += [(at_z(d), at_z(-d)) for d in RAW + WIDE]
     barrier = pltpu.get_barrier_semaphore()
-    known = jnp.int32(0)
-    for peers in routes:
-        for peer in peers:
-            pl.when(later(peer))(functools.partial(signal, barrier, peer))
-            known = known + jnp.where(later(peer), 0, 1)
-
-    @pl.when(known > 0)
-    def _():
-        pl.semaphore_wait(barrier, known)
-
-    for k, (_, source) in enumerate(routes):
-        pl.when(jnp.logical_not(later(source)))(functools.partial(signal, go.at[k], source))
-
-    def ready(k):
-        @pl.when(later(routes[k][0]))
-        def _():
-            pl.semaphore_wait(go.at[k], 1)
+    for peer in (at(-1), at_x(1), at_x(-1)):
+        signal(barrier, peer)
 
     def halo(b):
         return pltpu.make_async_remote_copy(
@@ -99,14 +79,6 @@
             device_id_type=MESH,
         )
 
-    follows = later(at(1))
-    loads[0].wait()
-
-    @pl.when((me < n - 1) & jnp.logical_not(follows))
-    def _():
-        for b in range(blocks):
-            halo(b).start()
-
     loads[2].wait()
     loads[3].wait()
 
@@ -135,21 +107,34 @@
             tf[top, LANES:] = turned * below
         return carry
 
-    def next_halo():
-        ready(0)
-
-        @pl.when((me < n - 1) & follows)
-        def _():
-            for b in range(blocks):
-                halo(b).start()
+    def tell_sides():
+        for d in (1, -1):
+            signal(steps.at[0], at_x(d))
+
+    def tell_next():
+        signal(steps.at[1], at_z(-1))
+        signal(steps.at[2], at_z(1))
+
+    edge = (iz == 0) | (iz == nz - 1)
 
     lax.fori_loop(0, 1, forward_table, 0)
-    next_halo()
+    loads[0].wait()
+    pl.semaphore_wait(barrier, 3)
+
+    @pl.when(me < n - 1)
+    def _():
+        for b in range(blocks):
+            halo(b).start()
+
+    @pl.when(me == n - 1)
+    def _():
+        signal(go, at(1))
+
+    @pl.when(me == 0)
+    def _():
+        pl.semaphore_wait(go, 1)
+
     lax.fori_loop(1, blocks, forward_table, 0)
-    ready(2)
-    ready(3)
-    for d in (1, -1):
-        signal(across, at_x(d))
 
     big_r = lax.broadcasted_iota(jnp.int32, (2 * ROWS, 2 * ROWS), 0)
     big_c = lax.broadcasted_iota(jnp.int32, (2 * ROWS, 2 * ROWS), 1)
@@ -193,6 +178,16 @@
             both = jnp.where(rows2 + cols2 >= LANES - 1, pair[:, :LANES], pair[:, LANES:])
             turned = pltpu.roll(both, 1, 1, stride=1, stride_axis=0)
             rx[ix, pl.ds(b * PER + k, 1), :] = jnp.sum(turned, axis=0, keepdims=True)
+        @pl.when(b == 0)
+        def _():
+            tell_sides()
+            pl.when(jnp.logical_not(edge))(tell_next)
+
+        @pl.when(b == 2)
+        def _():
+            pl.semaphore_wait(steps.at[0], 2)
+            pl.when(edge)(tell_next)
+
         return carry
 
     sacc[...] = jnp.zeros_like(sacc)
@@ -212,21 +207,17 @@
             src_ref=src, dst_ref=dst, send_sem=send, recv_sem=recv, device_id=ident(peer), device_id_type=MESH
         )
 
-    pl.semaphore_wait(across, 2)
     x_sends = [
         remote(rx.at[ix], rx.at[ix], x_send.at[d - 1], x_recv.at[d - 1], at_x(d)) for d in (2, 1, 3)
     ]
     for copy in x_sends:
         copy.start()
-
     back_c = remote(
         cce.at[pl.ds(0, ROWS)], cce.at[pl.ds(ROWS, ROWS)], back_send.at[0], back_recv.at[0], at(-1)
     )
     back_g = remote(
         gce.at[pl.ds(0, 16)], gce.at[pl.ds(ROWS, 16)], back_send.at[1], back_recv.at[1], at(-1)
     )
-
-    ready(1)
 
     @pl.when(me > 0)
     def _():
@@ -246,7 +237,11 @@
             tb[top, LANES:] = turned * strict
         return carry
 
+    pl.semaphore_wait(steps.at[1], 1)
     lax.fori_loop(0, blocks, backward_table, 0)
+    pl.semaphore_wait(steps.at[2], 1)
+    signal(steps.at[3], at_z(-2))
+    signal(steps.at[4], at_z(2))
 
     for d in range(1, nx):
         source = lax.rem(ix - d + nx, nx)
@@ -256,18 +251,22 @@
         total = total + rx[k]
     xs[...] = total.astype(BF16)
     z_sends = [remote(xs, rz.at[k], z_send.at[k], z_recv.at[k], at_z(d)) for k, d in enumerate(RAW)]
-    for k, copy in enumerate(z_sends):
-        ready(4 + k)
-        copy.start()
+    z_sends[0].start()
+    z_sends[1].start()
+    pl.semaphore_wait(steps.at[3], 1)
+    z_sends[2].start()
+    pl.semaphore_wait(steps.at[4], 1)
+    signal(steps.at[5], at_z(4))
     for copy in z_sends:
         copy.wait_recv()
     window = (total + rz[0].astype(F32)) + (rz[1].astype(F32) + rz[2].astype(F32))
     win[...] = window.astype(BF16)
     tot_ref[...] = window
     w_sends = [remote(win, rw.at[k], w_send.at[k], w_recv.at[k], at_z(d)) for k, d in enumerate(WIDE)]
-    for k, copy in enumerate(w_sends):
-        ready(4 + len(RAW) + k)
+    for copy in w_sends[:2]:
         copy.start()
+    pl.semaphore_wait(steps.at[5], 1)
+    w_sends[2].start()
 
     @pl.when(me < n - 1)
     def _():
@@ -375,8 +374,8 @@
             dma((len(RAW),)),
             dma((len(WIDE),)),
             dma((len(WIDE),)),
-            pltpu.SemaphoreType.REGULAR((4 + len(RAW) + len(WIDE),)),
             pltpu.SemaphoreType.REGULAR,
+            pltpu.SemaphoreType.REGULAR((6,)),
         ],
         compiler_params=pltpu.CompilerParams(collective_id=0, has_side_effects=True),
     )(inputs, upstream, medium_filter, short_filter.T)

time: 40.5 us -> 37.4 us (0.923)
  the two profiles are of different devices: /device:TPU:66 before, /device:TPU:96 now
where the time goes in v3:
time: 37.4 us; the launch traced here: 37.3 us
  Pallas kernels  36.6 us (98%)
  between operations  0.64 us (2%)
    pallas_call x1, Pallas kernels, local(): pl.pallas_call(functools.partial(kernel, nx, nz), out_shape=(vmem((rows,...  35.9 us

profile of v3, /device:TPU:96, one launch (start us, length us, event | category | flops | bytes accessed | tf_op | source)
XLA Modules:
  0.0 37.3 jit_solution(9709669955930284657)
XLA Ops:
  0.6 35.9 %shard_map.67 = (bf16[128,512]{1,0:T(8,128)(2,1)S(1)}, f32[40,128]{1,0:T(8,128)S(1)}) custom-call(bf16[128,512]{1,0:T(8,128)(2,1)} %x_hbm.1, bf16[128,512]{1,0:T(8,128)(2,1)} %up_hbm.1, bf16[32,128]{1,0:T(8,128)(2,1)} %med_hbm.1, bf16[7,32]{1,0:T(8,128)(2,1)} %bitcast.2), custom_call_target="tpu_custom_call" | custom-call | tf_op jit(solution)/shard_map/pallas_call | solution.py:342
  36.6 0.7 %shard_map.68 = (bf16[128,512]{1,0:T(8,128)(2,1)}, f32[32,128]{1,0:T(8,128)}, f32[7,32]{1,0:T(8,128)}) custom-call(bf16[128,512]{1,0:T(8,128)(2,1)S(1)} %get-tuple-element.8.ig_ref, f32[40,128]{1,0:T(8,128)S(1)} %get-tuple-element.9.tot_ref), custom_call_target="tpu_custom_call" | custom-call | tf_op jit(solution)/shard_map/pallas_call | solution.py:383

commit v4 on v3

--- a/solution.py
+++ b/solution.py
@@ -24,7 +24,7 @@
 
 def kernel(
     nx, nz, x_hbm, up_hbm, med_hbm, short_hbm, igv, tot_ref,
-    xe, upv, med_ref, short_ref, cce, gce, tf, tb, mrev, mfwd, sch, xf, sacc,
+    xe, upv, med_ref, short_ref, cce, gce, tf, tb, mrev, mfwd, sch, xf, sacc, pick,
     rx, xs, rz, win, rw,
     load_sem, halo_send, halo_recv, back_send, back_recv,
     x_send, x_recv, z_send, z_recv, w_send, w_recv, go, steps,
@@ -79,6 +79,18 @@
             device_id_type=MESH,
         )
 
+    loads[0].wait()
+    pl.semaphore_wait(barrier, 3)
+
+    @pl.when(me < n - 1)
+    def _():
+        for b in range(blocks):
+            halo(b).start()
+
+    @pl.when(me == n - 1)
+    def _():
+        signal(go, at(1))
+
     loads[2].wait()
     loads[3].wait()
 
@@ -117,24 +129,15 @@
 
     edge = (iz == 0) | (iz == nz - 1)
 
-    lax.fori_loop(0, 1, forward_table, 0)
-    loads[0].wait()
-    pl.semaphore_wait(barrier, 3)
-
-    @pl.when(me < n - 1)
-    def _():
-        for b in range(blocks):
-            halo(b).start()
-
-    @pl.when(me == n - 1)
-    def _():
-        signal(go, at(1))
+    lax.fori_loop(0, blocks, forward_table, 0)
 
     @pl.when(me == 0)
     def _():
         pl.semaphore_wait(go, 1)
 
-    lax.fori_loop(1, blocks, forward_table, 0)
+    tall_r = lax.broadcasted_iota(jnp.int32, (width, LANES), 0) // GROUP
+    tall_c = lax.broadcasted_iota(jnp.int32, (width, LANES), 1)
+    pick[...] = (tall_r == tall_c).astype(BF16)
 
     big_r = lax.broadcasted_iota(jnp.int32, (2 * ROWS, 2 * ROWS), 0)
     big_c = lax.broadcasted_iota(jnp.int32, (2 * ROWS, 2 * ROWS), 1)
@@ -193,14 +196,13 @@
     sacc[...] = jnp.zeros_like(sacc)
     lax.fori_loop(0, blocks, block, 0)
 
-    tall_r = lax.broadcasted_iota(jnp.int32, (width, LANES), 0) // GROUP
-    tall_c = lax.broadcasted_iota(jnp.int32, (width, LANES), 1)
-    rx[ix, groups : groups + 8, :] = jnp.dot(
-        sacc[...],
-        (tall_r == tall_c).astype(F32),
-        preferred_element_type=F32,
-        precision=lax.Precision.HIGHEST,
-    )
+    sums = sacc[...]
+    top = sums.astype(BF16)
+    rest = sums - top.astype(F32)
+    middle = rest.astype(BF16)
+    low = (rest - middle.astype(F32)).astype(BF16)
+    pieces = [jnp.dot(p, pick[...], preferred_element_type=F32) for p in (top, middle, low)]
+    rx[ix, groups : groups + 8, :] = pieces[0] + (pieces[1] + pieces[2])
 
     def remote(src, dst, send, recv, peer):
         return pltpu.make_async_remote_copy(
@@ -358,6 +360,7 @@
             vmem((8, width), F32),
             vmem((ROWS + 16, LANES), F32),
             vmem((8, width), F32),
+            vmem((width, LANES), BF16),
             vmem((nx, height, LANES), F32),
             vmem((height, LANES), BF16),
             vmem((len(RAW), height, LANES), BF16),

time: 37.4 us -> 37.2 us (level)
  the two profiles are of different devices: /device:TPU:96 before, /device:TPU:72 now
where the time goes in v4:
time: 37.2 us; the launch traced here: 37.1 us
  Pallas kernels  36.4 us (98%)
  between operations  0.64 us (2%)
    pallas_call x1, Pallas kernels, local(): pl.pallas_call(functools.partial(kernel, nx, nz), out_shape=(vmem((rows,...  35.7 us

profile of v4, /device:TPU:72, one launch (start us, length us, event | category | flops | bytes accessed | tf_op | source)
XLA Modules:
  0.0 37.1 jit_solution(11311527554533151903)
XLA Ops:
  0.6 35.7 %shard_map.67 = (bf16[128,512]{1,0:T(8,128)(2,1)S(1)}, f32[40,128]{1,0:T(8,128)S(1)}) custom-call(bf16[128,512]{1,0:T(8,128)(2,1)} %x_hbm.1, bf16[128,512]{1,0:T(8,128)(2,1)} %up_hbm.1, bf16[32,128]{1,0:T(8,128)(2,1)} %med_hbm.1, bf16[7,32]{1,0:T(8,128)(2,1)} %bitcast.2), custom_call_target="tpu_custom_call" | custom-call | tf_op jit(solution)/shard_map/pallas_call | solution.py:344
  36.4 0.7 %shard_map.68 = (bf16[128,512]{1,0:T(8,128)(2,1)}, f32[32,128]{1,0:T(8,128)}, f32[7,32]{1,0:T(8,128)}) custom-call(bf16[128,512]{1,0:T(8,128)(2,1)S(1)} %get-tuple-element.8.ig_ref, f32[40,128]{1,0:T(8,128)S(1)} %get-tuple-element.9.tot_ref), custom_call_target="tpu_custom_call" | custom-call | tf_op jit(solution)/shard_map/pallas_call | solution.py:386

commit v5 on v4

--- a/solution.py
+++ b/solution.py
@@ -25,7 +25,7 @@
 def kernel(
     nx, nz, x_hbm, up_hbm, med_hbm, short_hbm, igv, tot_ref,
     xe, upv, med_ref, short_ref, cce, gce, tf, tb, mrev, mfwd, sch, xf, sacc, pick,
-    rx, xs, rz, win, rw,
+    part_sum, rx, xs, rz, win, rw,
     load_sem, halo_send, halo_recv, back_send, back_recv,
     x_send, x_recv, z_send, z_recv, w_send, w_recv, go, steps,
 ):
@@ -180,7 +180,7 @@
             pair = nt(part, x_rev)
             both = jnp.where(rows2 + cols2 >= LANES - 1, pair[:, :LANES], pair[:, LANES:])
             turned = pltpu.roll(both, 1, 1, stride=1, stride_axis=0)
-            rx[ix, pl.ds(b * PER + k, 1), :] = jnp.sum(turned, axis=0, keepdims=True)
+            part_sum[pl.ds(b * PER + k, 1), :] = jnp.sum(turned, axis=0, keepdims=True)
         @pl.when(b == 0)
         def _():
             tell_sides()
@@ -202,7 +202,8 @@
     middle = rest.astype(BF16)
     low = (rest - middle.astype(F32)).astype(BF16)
     pieces = [jnp.dot(p, pick[...], preferred_element_type=F32) for p in (top, middle, low)]
-    rx[ix, groups : groups + 8, :] = pieces[0] + (pieces[1] + pieces[2])
+    part_sum[groups : groups + 8, :] = pieces[0] + (pieces[1] + pieces[2])
+    rx[ix] = part_sum[...].astype(BF16)
 
     def remote(src, dst, send, recv, peer):
         return pltpu.make_async_remote_copy(
@@ -248,9 +249,9 @@
     for d in range(1, nx):
         source = lax.rem(ix - d + nx, nx)
         remote(rx.at[ix], rx.at[source], x_send.at[d - 1], x_recv.at[d - 1], at_x(d)).wait_recv()
-    total = rx[0]
-    for k in range(1, nx):
-        total = total + rx[k]
+    total = part_sum[...]
+    for d in range(1, nx):
+        total = total + rx[lax.rem(ix + d, nx)].astype(F32)
     xs[...] = total.astype(BF16)
     z_sends = [remote(xs, rz.at[k], z_send.at[k], z_recv.at[k], at_z(d)) for k, d in enumerate(RAW)]
     z_sends[0].start()
@@ -361,7 +362,8 @@
             vmem((ROWS + 16, LANES), F32),
             vmem((8, width), F32),
             vmem((width, LANES), BF16),
-            vmem((nx, height, LANES), F32),
+            vmem((height, LANES), F32),
+            vmem((nx, height, LANES), BF16),
             vmem((height, LANES), BF16),
             vmem((len(RAW), height, LANES), BF16),
             vmem((height, LANES), BF16),

time: 37.2 us -> 37.2 us (level)
  the two profiles are of different devices: /device:TPU:72 before, /device:TPU:96 now
where the time goes in v5:
time: 37.2 us; the launch traced here: 37.1 us
  Pallas kernels  36.4 us (98%)
  between operations  0.64 us (2%)
    pallas_call x1, Pallas kernels, local(): pl.pallas_call(functools.partial(kernel, nx, nz), out_shape=(vmem((rows,...  35.7 us

profile of v5, /device:TPU:96, one launch (start us, length us, event | category | flops | bytes accessed | tf_op | source)
XLA Modules:
  0.0 37.1 jit_solution(3097316949802713690)
XLA Ops:
  0.6 35.7 %shard_map.67 = (bf16[128,512]{1,0:T(8,128)(2,1)S(1)}, f32[40,128]{1,0:T(8,128)S(1)}) custom-call(bf16[128,512]{1,0:T(8,128)(2,1)} %x_hbm.1, bf16[128,512]{1,0:T(8,128)(2,1)} %up_hbm.1, bf16[32,128]{1,0:T(8,128)(2,1)} %med_hbm.1, bf16[7,32]{1,0:T(8,128)(2,1)} %bitcast.2), custom_call_target="tpu_custom_call" | custom-call | tf_op jit(solution)/shard_map/pallas_call | solution.py:345
  36.4 0.7 %shard_map.68 = (bf16[128,512]{1,0:T(8,128)(2,1)}, f32[32,128]{1,0:T(8,128)}, f32[7,32]{1,0:T(8,128)}) custom-call(bf16[128,512]{1,0:T(8,128)(2,1)S(1)} %get-tuple-element.8.ig_ref, f32[40,128]{1,0:T(8,128)S(1)} %get-tuple-element.9.tot_ref), custom_call_target="tpu_custom_call" | custom-call | tf_op jit(solution)/shard_map/pallas_call | solution.py:388
